TPU v7x, 32 devices: a whole 2x2x4 slice. The times are simulated.
32 devices in a mesh: row: 4 (over x, core), col: 8 (over z, y).
Axes of the slice: x: 2, y: 2, z: 4, core: 2. Of those that a mesh axis runs over, the one named last changes fastest.
Arguments:
- green_vectors: float32 [512, 131072], P('row', 'col'), may hold values from -6 to 6
- amplitudes: float32 [2048, 131072], P('row', 'col'), may hold values from -0.015625 to 0.015625
- cholesky: float32 [2048, 4096], P(('row', 'col')), may hold values from -0.125 to 0.125
Outputs:
- force_bias: float32 [512, 4096], P('col', 'row')
All inputs are finite; a program needn't handle non-finite values.
Results may differ from a plain program's by a relative error of at most 0.000084.
Values sent between devices are 32-bit elements; how exact they have to be, the bound alone decides.
A program may use at most 128 MiB of HBM per device.

v0:
```python
import functools

import jax
import jax.numpy as jnp
from jax import lax
from jax.experimental import pallas as pl
from jax.experimental.pallas import tpu as pltpu
from jax.sharding import PartitionSpec as P

SHARES = (6, 5, 3, 2)
MESH = pl.DeviceIdType.MESH


def three_pass(left, right, dims):
    return lax.dot_general(
        left,
        right,
        (dims, ((), ())),
        precision=lax.Precision.HIGH,
        preferred_element_type=jnp.float32,
    )


def halves(x):
    high = x.astype(jnp.bfloat16)
    return high, (x - high.astype(jnp.float32)).astype(jnp.bfloat16)


def tail_kernel(
    rows, cols, total, chol, out, landed, slab, leaving, arrived,
    send_sem, recv_sem, load_sem, row_send, row_recv,
):
    row, col = lax.axis_index("row"), lax.axis_index("col")
    quarter = out.shape[1]
    walkers = out.shape[0]

    barrier = pltpu.get_barrier_semaphore()
    for k in range(1, cols):
        pl.semaphore_signal(barrier, inc=1, device_id=(row, lax.rem(col + k, cols)), device_id_type=MESH)
    for m in range(1, rows):
        pl.semaphore_signal(barrier, inc=1, device_id=(lax.rem(row + m, rows), col), device_id_type=MESH)
    order = [rows // 2] + [m for m in range(1, rows) if m != rows // 2] + [0]
    loads = {}
    for m in order:
        start = pl.multiple_of(lax.rem(row + m, rows) * quarter, quarter)
        loads[m] = pltpu.make_async_copy(chol.at[:, pl.ds(start, quarter)], slab.at[m], load_sem.at[m])
    own = pltpu.make_async_copy(total.at[col], landed.at[0], recv_sem.at[0])
    own.start()
    for m in order:
        loads[m].start()
    pl.semaphore_wait(barrier, rows + cols - 2)

    copies = []
    for k in range(1, cols):
        target = lax.rem(col + k, cols)
        copy = pltpu.make_async_remote_copy(
            src_ref=total.at[target],
            dst_ref=landed.at[k],
            send_sem=send_sem.at[k],
            recv_sem=recv_sem.at[k],
            device_id=(row, target),
            device_id_type=MESH,
        )
        copy.start()
        copies.append(copy)
    own.wait()
    effective = landed[0]
    for k, copy in enumerate(copies):
        copy.wait_recv()
        effective = effective + landed[k + 1]
    high, low = halves(effective)
    both = jnp.concatenate([high, low], axis=0)

    tile = min(512, quarter)
    sends = []
    for m in order:
        loads[m].wait()
        for t in range(0, quarter, tile):
            right_high, right_low = halves(slab[m, :, t : t + tile])
            pair = jnp.dot(both, right_high, preferred_element_type=jnp.float32)
            rest = jnp.dot(high, right_low, preferred_element_type=jnp.float32)
            leaving[m, :, t : t + tile] = pair[:walkers] + (pair[walkers:] + rest)
        if m:
            send = pltpu.make_async_remote_copy(
                src_ref=leaving.at[m],
                dst_ref=arrived.at[m],
                send_sem=row_send.at[m],
                recv_sem=row_recv.at[m],
                device_id=(lax.rem(row + m, rows), col),
                device_id_type=MESH,
            )
            send.start()
            sends.append((m, send))
    result = leaving[0]
    for m, send in sends:
        send.wait_recv()
        result = result + arrived[m]
    out[...] = result
    for copy in copies:
        copy.wait_send()
    for m, send in sends:
        send.wait_send()


def tail(total, chol):
    rows, cols = lax.axis_size("row"), lax.axis_size("col")
    walkers, depth = total.shape[0] // cols, total.shape[1]
    quarter = chol.shape[1] // rows
    f32 = jnp.float32
    return pl.pallas_call(
        functools.partial(tail_kernel, rows, cols),
        out_shape=jax.ShapeDtypeStruct((walkers, quarter), f32),
        in_specs=[pl.BlockSpec(memory_space=pl.ANY)] * 2,
        out_specs=pl.BlockSpec(memory_space=pltpu.VMEM),
        scratch_shapes=[
            pltpu.VMEM((cols, walkers, depth), f32),
            pltpu.VMEM((rows, depth, quarter), f32),
            pltpu.VMEM((rows, walkers, quarter), f32),
            pltpu.VMEM((rows, walkers, quarter), f32),
            pltpu.SemaphoreType.DMA((cols,)),
            pltpu.SemaphoreType.DMA((cols,)),
            pltpu.SemaphoreType.DMA((rows,)),
            pltpu.SemaphoreType.DMA((rows,)),
            pltpu.SemaphoreType.DMA((rows,)),
        ],
        compiler_params=pltpu.CompilerParams(
            collective_id=0, has_side_effects=True, vmem_limit_bytes=32 * 1024 * 1024
        ),
    )(total.reshape(cols, walkers, depth), chol)


def per_device(green_vectors, amplitudes, cholesky):
    rows = lax.axis_size("row")
    me = lax.axis_index("row")
    held, pairs = green_vectors.shape
    sibling = [(i, i ^ 1) for i in range(rows)]
    hops = range(2, rows, 2)
    cuts = [0]
    for share in SHARES:
        cuts.append(cuts[-1] + share * pairs // sum(SHARES))

    def part(array, c):
        return lax.slice_in_dim(array, cuts[c], cuts[c + 1], axis=1)

    def far(piece):
        return [lax.ppermute(piece, "row", [(i, (i + hop) % rows) for i in range(rows)]) for hop in hops]

    def terms(block, other, slab):
        return three_pass(jnp.concatenate([block, other], axis=0), slab, ((1,), (1,)))

    def cross(pieces):
        return [lax.ppermute(piece, "row", sibling) for piece in pieces]

    def dots(pieces, crossed, c):
        return [terms(a, b, part(amplitudes, c)) for a, b in zip(pieces, crossed)]

    first, second = far(part(green_vectors, 0)), far(part(green_vectors, 1))
    stacked = lax.all_gather(cholesky, "col", axis=0, tiled=True)
    near = lax.ppermute(green_vectors, "row", sibling)
    own = terms(green_vectors, near, amplitudes)
    piece, own = lax.optimization_barrier((part(green_vectors, 2), own))
    third = far(piece)
    second, own = lax.optimization_barrier((second, own))
    sums = dots(first, cross(first), 0)
    piece, sums = lax.optimization_barrier((part(green_vectors, 3), sums))
    fourth = far(piece)
    third, sums = lax.optimization_barrier((third, sums))
    for c, pieces in ((1, second), (2, third)):
        sums = [a + b for a, b in zip(sums, dots(pieces, cross(pieces), c))]
        if c == 2:
            fourth, sums, stacked = lax.optimization_barrier((fourth, sums, stacked))
    sums = [a + b for a, b in zip(sums, dots(fourth, cross(fourth), 3))]

    total = jnp.zeros((rows * held, amplitudes.shape[0]), jnp.float32)
    for at, block in enumerate([own] + sums):
        for side in range(2):
            owner = lax.rem(me - 2 * at + rows, rows) ^ side
            total = lax.dynamic_update_slice(
                total, lax.slice_in_dim(block, side * held, (side + 1) * held, axis=0), (owner * held, 0)
            )
    return tail(total, stacked)


def solution(mesh):
    placed = (P("row", "col"), P("row", "col"), P(("row", "col"), None))
    return jax.shard_map(
        per_device, mesh=mesh, in_specs=placed, out_specs=P("col", "row"), check_vma=False
    )
```

profile of v0, /device:TPU:13, one launch (start us, length us, event | category | flops | bytes accessed | tf_op | source)
XLA Modules:
  0.0 254.4 jit_solution(12749945163468311093)
XLA Ops:
  6.5 0.0 all-gather.2.cloned.1.call-start
  6.5 0.7 collective-permute-start.1
  7.2 0.0 all-gather.2.cloned.1.call-update
  7.3 2.1 slice.41
  9.4 1.3 collective-permute-start.2
  10.7 3.5 %slice.36 = f32[128,5120]{1,0:T(8,128)} slice(f32[128,16384]{1,0:T(8,128)} %param.3), slice={[0:128], [6144:11264]} | slice | bytes 5242880 | tf_op jit(solution)/shard_map/slice | solution.py:143
  14.2 0.3 collective-permute-start
  14.4 2.8 %slice.37 = f32[128,3072]{1,0:T(8,128)} slice(f32[128,16384]{1,0:T(8,128)} %param.3), slice={[0:128], [11264:14336]} | slice | bytes 3145728 | tf_op jit(solution)/shard_map/slice | solution.py:143
  17.2 61.4 %collective-permute-done.2 = f32[128,6144]{1,0:T(8,128)S(1)} collective-permute-done((f32[128,6144]{1,0:T(8,128)S(1)}, f32[128,6144]{1,0:T(8,128)S(1)}, u32[]{:S(2)}, u32[]{:S(2)}) %collective-permute-start.2) | collective-permute-done | bytes 3145760 | tf_op jit(solution)/shard_map/ppermute | solution.py:146
  78.5 2.6 %collective-permute-start.3 = (f32[128,6144]{1,0:T(8,128)S(1)}, f32[128,6144]{1,0:T(8,128)}, u32[]{:S(2)}, u32[]{:S(2)}) collective-permute-start(f32[128,6144]{1,0:T(8,128)S(1)} %collective-permute-done.2), channel_id=1, source_target_pairs={{0,8},{8,0},{16,24},{24,16},{1,9},{9,1},{17,25},{25,17},{2,10},{10... | collective-permute-start | bytes 9437192 | tf_op jit(solution)/shard_map/ppermute | solution.py:152
  81.1 0.0 collective-permute-done.1
  81.1 21.8 %fusion = f32[256,512]{1,0:T(8,128)} fusion(f32[512,16384]{1,0:T(8,128)} %param.4, f32[128,16384]{1,0:T(8,128)} %collective-permute-done.1, f32[128,16384]{1,0:T(8,128)} %param.3), kind=kOutput, calls=%fused_computation | convolution fusion | flops 12889096192 | bytes 50855936 | tf_op jit(solution)/shard_map/dot_general | solution.py:15
  102.9 31.8 %collective-permute-done = f32[128,5120]{1,0:T(8,128)} collective-permute-done((f32[128,5120]{1,0:T(8,128)}, f32[128,5120]{1,0:T(8,128)}, u32[]{:S(2)}, u32[]{:S(2)}) %collective-permute-start) | collective-permute-done | bytes 2621472 | tf_op jit(solution)/shard_map/ppermute | solution.py:146
  134.7 1.5 collective-permute-start.6
  136.3 1.2 collective-permute-start.5
  137.5 1.3 slice.40
  138.8 0.0 collective-permute-done.3
  138.8 9.6 %fusion.4 = f32[256,512]{1,0:T(8,128)S(1)} fusion(f32[512,16384]{1,0:T(8,128)} %param.4, f32[128,6144]{1,0:T(8,128)} %collective-permute-done.3, f32[128,6144]{1,0:T(8,128)S(1)} %collective-permute-done.2), kind=kOutput, calls=%fused_computation.4 | convolution fusion | flops 4833411072 | bytes 19398656 | tf_op jit(solution)/shard_map/dot_general | solution.py:15
  148.4 24.0 %collective-permute-done.5 = f32[128,3072]{1,0:T(8,128)S(1)} collective-permute-done((f32[128,3072]{1,0:T(8,128)}, f32[128,3072]{1,0:T(8,128)S(1)}, u32[]{:S(2)}, u32[]{:S(2)}) %collective-permute-start.5) | collective-permute-done | bytes 1572896 | tf_op jit(solution)/shard_map/ppermute | solution.py:146
  172.4 0.9 collective-permute-start.7
  173.3 1.2 collective-permute-start.4
  174.5 0.0 collective-permute-done.6
  174.5 8.5 %fusion.6 = f32[256,512]{1,0:T(8,128)S(1)} fusion(f32[512,16384]{1,0:T(8,128)} %param.4, f32[128,5120]{1,0:T(8,128)S(1)} %collective-permute-done.6, f32[128,5120]{1,0:T(8,128)} %collective-permute-done), kind=kOutput, calls=%fused_computation.6 | convolution fusion | flops 4027842560 | bytes 16252928 | tf_op jit(solution)/shard_map/dot_general | solution.py:15
  183.0 0.0 copy-start.1
  183.0 0.0 collective-permute-done.7
  183.0 5.5 %add_add_fusion = f32[256,512]{1,0:T(8,128)S(1)} fusion(f32[256,512]{1,0:T(8,128)S(1)} %fusion.4, f32[256,512]{1,0:T(8,128)S(1)} %fusion.6, f32[512,16384]{1,0:T(8,128)} %param.4, f32[128,3072]{1,0:T(8,128)S(1)} %collective-permute-done.7, f32[128,3072]{1,0:T(8,128)S(1)} %collective-permute-done.5), kind=kOutput, calls=%fused_computation.24 | convolution fusion | flops 2416967680 | bytes 11010048 | tf_op jit(solution)/shard_map/dot_general | solution.py:15
  188.6 9.4 %collective-permute-done.4 = f32[128,2048]{1,0:T(8,128)S(1)} collective-permute-done((f32[128,2048]{1,0:T(8,128)S(1)}, f32[128,2048]{1,0:T(8,128)S(1)}, u32[]{:S(2)}, u32[]{:S(2)}) %collective-permute-start.4) | collective-permute-done | bytes 1048608 | tf_op jit(solution)/shard_map/ppermute | solution.py:146
  198.0 0.0 all-gather.2.cloned.1.call-done.chol
  198.0 0.9 collective-permute-start.8
  198.9 0.1 broadcast_in_dim.3
  199.0 0.0 copy-done.1
  199.0 0.0 copy-start
  199.1 2.1 collective-permute-done.8
  201.1 4.2 %fusion.16 = f32[256,512]{1,0:T(8,128)S(1)} fusion(f32[512,16384]{1,0:T(8,128)} %param.4, f32[128,2048]{1,0:T(8,128)S(1)} %collective-permute-done.8, f32[128,2048]{1,0:T(8,128)S(1)} %collective-permute-done.4), kind=kOutput, calls=%fused_computation.16 | convolution fusion | flops 1611137024 | bytes 6815744 | tf_op jit(solution)/shard_map/dot_general | solution.py:15
  205.4 0.1 add.37
  205.5 0.0 copy-done
  205.6 41.3 %shard_map.37 = f32[64,1024]{1,0:T(8,128)S(1)} custom-call(f32[8,64,512]{2,1,0:T(8,128)S(1)} %bitcast.2, f32[512,4096]{1,0:T(8,128)S(1)} %copy-done), custom_call_target="tpu_custom_call" | custom-call | tf_op jit(solution)/shard_map/pallas_call | solution.py:110
  246.9 0.7 copy.9
  (4 shorter events, 0.1 us)
Async XLA Ops:
  6.5 191.5 %all-gather.2.cloned.1.call-start = ((), (), s32[]{:S(2)}) async-start(), calls=%async_computation | async-start | bytes 9437184 | tf_op jit(solution)/shard_map/all_gather | solution.py:158
  6.5 74.6 %collective-permute-start.1 = (f32[128,16384]{1,0:T(8,128)}, f32[128,16384]{1,0:T(8,128)}, u32[]{:S(2)}, u32[]{:S(2)}) collective-permute-start(f32[128,16384]{1,0:T(8,128)} %param.3), channel_id=1, source_target_pairs={{0,8},{8,0},{16,24},{24,16},{1,9},{9,1},{17,25},{25,17},{2,10},{10... | collective-permute-start | bytes 25165832 | tf_op jit(solution)/shard_map/ppermute | solution.py:159
  9.4 69.2 %collective-permute-start.2 = (f32[128,6144]{1,0:T(8,128)S(1)}, f32[128,6144]{1,0:T(8,128)S(1)}, u32[]{:S(2)}, u32[]{:S(2)}) collective-permute-start(f32[128,6144]{1,0:T(8,128)S(1)} %slice.41), channel_id=1, source_target_pairs={{0,16},{8,24},{16,0},{24,8},{1,17},{9,25},{17,1},{25,9},{2,18},{10... | collective-permute-start | bytes 9437192 | tf_op jit(solution)/shard_map/ppermute | solution.py:146
  14.2 120.6 %collective-permute-start = (f32[128,5120]{1,0:T(8,128)}, f32[128,5120]{1,0:T(8,128)}, u32[]{:S(2)}, u32[]{:S(2)}) collective-permute-start(f32[128,5120]{1,0:T(8,128)} %slice.36), channel_id=1, source_target_pairs={{0,16},{8,24},{16,0},{24,8},{1,17},{9,25},{17,1},{25,9},{2,18},{10... | collective-permute-start | bytes 7864328 | tf_op jit(solution)/shard_map/ppermute | solution.py:146
  78.5 60.2 %collective-permute-start.3 = (f32[128,6144]{1,0:T(8,128)S(1)}, f32[128,6144]{1,0:T(8,128)}, u32[]{:S(2)}, u32[]{:S(2)}) collective-permute-start(f32[128,6144]{1,0:T(8,128)S(1)} %collective-permute-done.2), channel_id=1, source_target_pairs={{0,8},{8,0},{16,24},{24,16},{1,9},{9,1},{17,25},{25,17},{2,10},{10... | collective-permute-start | bytes 9437192 | tf_op jit(solution)/shard_map/ppermute | solution.py:152
  134.7 39.8 %collective-permute-start.6 = (f32[128,5120]{1,0:T(8,128)}, f32[128,5120]{1,0:T(8,128)S(1)}, u32[]{:S(2)}, u32[]{:S(2)}) collective-permute-start(f32[128,5120]{1,0:T(8,128)} %collective-permute-done), channel_id=1, source_target_pairs={{0,8},{8,0},{16,24},{24,16},{1,9},{9,1},{17,25},{25,17},{2,10},{10... | collective-permute-start | bytes 7864328 | tf_op jit(solution)/shard_map/ppermute | solution.py:152
  136.3 36.2 %collective-permute-start.5 = (f32[128,3072]{1,0:T(8,128)}, f32[128,3072]{1,0:T(8,128)S(1)}, u32[]{:S(2)}, u32[]{:S(2)}) collective-permute-start(f32[128,3072]{1,0:T(8,128)} %slice.37), channel_id=1, source_target_pairs={{0,16},{8,24},{16,0},{24,8},{1,17},{9,25},{17,1},{25,9},{2,18},{10... | collective-permute-start | bytes 4718600 | tf_op jit(solution)/shard_map/ppermute | solution.py:146
  172.4 10.6 %collective-permute-start.7 = (f32[128,3072]{1,0:T(8,128)S(1)}, f32[128,3072]{1,0:T(8,128)S(1)}, u32[]{:S(2)}, u32[]{:S(2)}) collective-permute-start(f32[128,3072]{1,0:T(8,128)S(1)} %collective-permute-done.5), channel_id=1, source_target_pairs={{0,8},{8,0},{16,24},{24,16},{1,9},{9,1},{17,25},{25,17},{2,10},{10... | collective-permute-start | bytes 4718600 | tf_op jit(solution)/shard_map/ppermute | solution.py:152
  173.3 24.7 %collective-permute-start.4 = (f32[128,2048]{1,0:T(8,128)S(1)}, f32[128,2048]{1,0:T(8,128)S(1)}, u32[]{:S(2)}, u32[]{:S(2)}) collective-permute-start(f32[128,2048]{1,0:T(8,128)S(1)} %slice.40), channel_id=1, source_target_pairs={{0,16},{8,24},{16,0},{24,8},{1,17},{9,25},{17,1},{25,9},{2,18},{10... | collective-permute-start | bytes 3145736 | tf_op jit(solution)/shard_map/ppermute | solution.py:146
  183.0 16.0 %copy-start.1 = (f32[256,512]{1,0:T(8,128)S(1)}, f32[256,512]{1,0:T(8,128)}, u32[]{:S(2)}) copy-start(f32[256,512]{1,0:T(8,128)} %fusion) | copy-start | bytes 1572868
  198.0 3.1 %collective-permute-start.8 = (f32[128,2048]{1,0:T(8,128)S(1)}, f32[128,2048]{1,0:T(8,128)S(1)}, u32[]{:S(2)}, u32[]{:S(2)}) collective-permute-start(f32[128,2048]{1,0:T(8,128)S(1)} %collective-permute-done.4), channel_id=1, source_target_pairs={{0,8},{8,0},{16,24},{24,16},{1,9},{9,1},{17,25},{25,17},{2,10},{10... | collective-permute-start | bytes 3145736 | tf_op jit(solution)/shard_map/ppermute | solution.py:152
  199.0 6.6 %copy-start = (f32[512,4096]{1,0:T(8,128)S(1)}, f32[512,4096]{1,0:T(8,128)}, u32[]{:S(2)}) copy-start(f32[512,4096]{1,0:T(8,128)} %all-gather.2.cloned.1.call-done.chol) | copy-start | bytes 25165828
Sparse Core Ops, SparseCore 0:
  9.5 122.2 all-gather.1
where the time goes:
time: 255 us; the launch traced here: 254 us
  waiting for transfers between devices  129 us (51%)
  matrix products  49.7 us (19%)
  Pallas kernels  41.3 us (16%)
  between operations  13.5 us (5%)
  local copies, waits for them, and re-layouts  10.6 us (4%)
  starting transfers between devices  10.4 us (4%)
    ppermute x4, waiting for transfers between devices, far(): lax.ppermute(piece, 'row', [(i, (i + hop) % rows) for i in range(rows)])  127 us
    dot_general x5, matrix products, three_pass(): lax.dot_general(left, right, (dims, ((), ())), precision=lax.Precision.HI...  49.7 us
    pallas_call x1, Pallas kernels, tail(): pl.pallas_call(functools.partial(tail_kernel, rows, cols), out_shape=jax....  41.3 us
    slice x4, local copies, waits for them, and re-layouts, part(): return lax.slice_in_dim(array, cuts[c], cuts[c + 1], axis=1)  9.67 us
    ppermute x4, starting transfers between devices, cross(): return [lax.ppermute(piece, 'row', sibling) for piece in pieces]  5.81 us
  transfers between devices with their start and end apart: 10, of which 5 were waited for; matrix products, arithmetic and copies ran while one was open for 22% of the time, Pallas kernels for 0%

commit v1 on v0

v1 whole, which is shorter than its diff:
```python
import functools

import jax
import jax.numpy as jnp
from jax import lax
from jax.experimental import pallas as pl
from jax.experimental.pallas import tpu as pltpu
from jax.sharding import PartitionSpec as P

MESH = pl.DeviceIdType.MESH
F32, BF16 = jnp.float32, jnp.bfloat16
ROWS = 8
SLOTS = 4
CHUNK = 2048
TILE = 512


def halves(x):
    high = x.astype(BF16)
    return high, (x - high.astype(F32)).astype(BF16)


def dot_nt(left, right):
    return lax.dot_general(left, right, (((1,), (1,)), ((), ())), preferred_element_type=F32)


def dot_nn(left, right):
    return jnp.dot(left, right, preferred_element_type=F32)


def kernel(
    rows, cols, g, a, c, out, near, cbuf,
    ahi, alo, chi, clo, xs, ss, at, gt, ct, eown, acc, acc2, stage, eland, esend, esib, fbs, fbl,
    x_send, x_recv, f_send, f_recv, x_free, s_free, n_send, n_recv, ld,
    cl_sem, cs_send, cs_recv, c_send, c_recv, r_send, r_recv, ct_sem,
    e_send, e_recv, es_send, es_recv, fb_send, fb_recv,
):
    row, col = lax.axis_index("row"), lax.axis_index("col")
    sib = row + 1 - 2 * lax.rem(row, 2)
    far = lax.rem(row + rows // 2, rows)
    far_sib = lax.rem(sib + rows // 2, rows)
    pal = col + 1 - 2 * lax.rem(col, 2)
    opr, ng, _, pairs = g.shape
    depth = a.shape[0]
    held, wpo = opr * ng * ROWS, ng * ROWS
    chunk, nkc = ahi.shape[2], ahi.shape[0]
    tile = at.shape[2]
    per = chunk // tile
    cr, quarter = c.shape[0], c.shape[1] // rows
    npeer = cols // 2
    slots = xs.shape[0]
    n = 2 * opr * ROWS

    def remote(src, dst, send, recv, target):
        return pltpu.make_async_remote_copy(
            src_ref=src, dst_ref=dst, send_sem=send, recv_sem=recv, device_id=target, device_id_type=MESH
        )

    def loop(lo, hi, body):
        def step(i, carry):
            body(i)
            return carry

        lax.fori_loop(lo, hi, step, 0)

    barrier = pltpu.get_barrier_semaphore()
    pl.semaphore_signal(barrier, inc=1, device_id=(far, col), device_id_type=MESH)
    pl.semaphore_signal(barrier, inc=1, device_id=(sib, col), device_id_type=MESH)

    @functools.partial(loop, 1, cols)
    def _(t):
        pl.semaphore_signal(barrier, inc=1, device_id=(row, lax.rem(col + t, cols)), device_id_type=MESH)

    def load(i, slot):
        at_pairs = pl.ds(pl.multiple_of(i * tile, tile), tile)
        return [
            pltpu.make_async_copy(a.at[:, at_pairs], at.at[slot], ld.at[slot, 0]),
            pltpu.make_async_copy(g.at[:, :, :, at_pairs], gt.at[slot, 0], ld.at[slot, 1]),
            pltpu.make_async_copy(near.at[:, :, :, at_pairs], gt.at[slot, 1], ld.at[slot, 2]),
        ]

    for copy in load(0, 0)[:2]:
        copy.start()
    local = [
        pltpu.make_async_copy(
            c.at[:, pl.ds(pl.multiple_of(quarter_of * quarter, quarter), quarter)], cbuf.at[col, 0, h], cl_sem.at[h]
        )
        for h, quarter_of in enumerate((far, row))
    ]
    pl.semaphore_wait(barrier, cols + 1)

    def pairs_of(k):
        return pl.ds(pl.multiple_of(k * chunk, chunk), chunk)

    def x_copy(j, k):
        slot = lax.rem(j, slots)
        return remote(
            g.at[:, j, :, pairs_of(k)], xs.at[slot, :, :, pairs_of(k)],
            x_send.at[slot, k], x_recv.at[slot, k], (far, col),
        )

    def f_copy(j, k):
        slot = lax.rem(j, slots)
        return remote(
            xs.at[slot, :, :, pairs_of(k)], ss.at[slot, :, :, pairs_of(k)],
            f_send.at[slot, k], f_recv.at[slot, k], (sib, col),
        )

    def n_copy(k):
        return remote(g.at[:, :, :, pairs_of(k)], near.at[:, :, :, pairs_of(k)], n_send.at[k], n_recv.at[k], (sib, col))

    loop(0, nkc, lambda k: x_copy(0, k).start())
    n_copy(0).start()

    def c_quarter(m):
        return c.at[:, pl.ds(pl.multiple_of(m * quarter, quarter), quarter)]

    to_sib = [
        remote(c_quarter(m), cbuf.at[col, 1, h], cs_send.at[h], cs_recv.at[h], (sib, col))
        for h, m in enumerate((far_sib, sib))
    ]

    def c_target(p):
        return jnp.where(p == 0, pal, lax.rem(col + 2 * p, cols))

    def c_source(p):
        return jnp.where(p == 0, pal, lax.rem(col + cols - 2 * p, cols))

    def c_copies(p):
        target = (row, c_target(p))
        return [
            remote(c_quarter(far), cbuf.at[col, 0, 0], c_send.at[p, 0], c_recv.at[p, 0], target),
            remote(c_quarter(row), cbuf.at[col, 0, 1], c_send.at[p, 1], c_recv.at[p, 1], target),
            remote(cbuf.at[col, 1], cbuf.at[col, 1], c_send.at[p, 2], c_recv.at[p, 2], target),
        ]

    def r_copy(p):
        return remote(cbuf.at[c_source(p)], cbuf.at[c_source(p)], r_send.at[p], r_recv.at[p], (row, pal))

    for copy in to_sib:
        copy.start()
    loop(1, nkc, lambda k: n_copy(k).start())

    def send_own(p):
        for copy in c_copies(p)[:2]:
            copy.start()

    loop(0, npeer, send_own)
    for copy in local:
        copy.start()
    for j in range(1, min(slots, ng)):
        loop(0, nkc, functools.partial(lambda j, k: x_copy(j, k).start(), j))
    for copy in to_sib:
        copy.wait_recv()
    loop(0, npeer, lambda p: c_copies(p)[2].start())

    def relay(p):
        for copy in c_copies(p):
            copy.wait_recv()
        r_copy(p).start()

    eown[...] = jnp.zeros_like(eown)
    n_copy(0).wait_recv()
    load(0, 0)[2].start()

    @functools.partial(loop, 0, nkc)
    def _(kk):
        for q in range(per):
            slot = q % 2
            i = kk * per + q
            if q + 1 < per:
                for copy in load(i + 1, 1 - slot):
                    copy.start()
            else:

                @pl.when(kk + 1 < nkc)
                def _():
                    n_copy(kk + 1).wait_recv()
                    for copy in load(i + 1, 1 - slot):
                        copy.start()

            for copy in load(i, slot):
                copy.wait()
            high, low = halves(at[slot])
            ahi[kk, :, q * tile : (q + 1) * tile] = high
            alo[kk, :, q * tile : (q + 1) * tile] = low
            g_high, g_low = halves(gt[slot].reshape(2 * held, tile))
            pair = dot_nt(jnp.concatenate([g_high, g_low], axis=0), high)
            eown[...] += pair[: 2 * held] + (pair[2 * held :] + dot_nt(g_high, low))

    def steps(j, lo, hi):
        slot = lax.rem(j, slots)

        @functools.partial(loop, lo, hi)
        def _(k):
            @pl.when(k < nkc)
            def _():
                x_copy(j, k).wait_recv()
                f_copy(j, k).start()

            @pl.when(k > 0)
            def _():
                f_copy(j, k - 1).wait_recv()
                here = pairs_of(k - 1)
                block = jnp.concatenate(
                    [
                        xs[slot, :, :, here].reshape(n // 2, chunk),
                        ss[slot, :, :, here].reshape(n // 2, chunk),
                    ],
                    axis=0,
                )
                high, low = halves(block)
                acc[...] += dot_nt(jnp.concatenate([high, low], axis=0), ahi[k - 1])
                acc2[...] += dot_nt(high, alo[k - 1])

    def clear():
        acc[...] = jnp.zeros_like(acc)
        acc2[...] = jnp.zeros_like(acc2)

    def e_copy(j, t):
        target = lax.rem(col + t, cols)
        return remote(stage.at[j, target], eland.at[j, t], e_send.at[j, t], e_recv.at[j, t], (row, target))

    def es_copy(j):
        return remote(esend.at[j], esib.at[j], es_send.at[j], es_recv.at[j], (sib, col))

    def scatter(j):
        for i in range(opr):
            mine = pl.multiple_of(i * wpo + j * ROWS, ROWS)
            stage[j, row * opr + i] = eown[pl.ds(mine, ROWS)]
            stage[j, sib * opr + i] = eown[pl.ds(held + mine, ROWS)]
            at_far, at_sib = slice(i * ROWS, (i + 1) * ROWS), slice((opr + i) * ROWS, (opr + i + 1) * ROWS)
            for owner, here in ((far, at_far), (far_sib, at_sib)):
                below = slice(n + here.start, n + here.stop)
                stage[j, owner * opr + i] = acc[here] + (acc[below] + acc2[here])
        loop(1, cols, lambda t: e_copy(j, t).start())

    def gather(j):
        def add(t, total):
            e_copy(j, t).wait_recv()
            return total + eland[j, t]

        esend[j] = lax.fori_loop(1, cols, add, stage[j, col])
        es_copy(j).start()

    def fb_copy(first, last):
        return remote(
            fbs.at[pl.ds(first, last - first)], fbl.at[pl.ds(first, last - first)],
            fb_send.at[first], fb_recv.at[first], (far, col),
        )

    def bias(first, last):
        m = (last - first) * ROWS

        def part(ref):
            high, low = halves(ref[first:last].reshape(m, depth))
            return jnp.concatenate([high, low], axis=0), high

        def term(both, high, q, h):
            here = slice(h * quarter, (h + 1) * quarter)
            pair = dot_nn(both, chi[q, :, here])
            return pair[:m] + (pair[m:] + dot_nn(high, clo[q, :, here]))

        mine = part(esend)
        away = term(*mine, 0, 0)
        for j in range(first, last):
            es_copy(j).wait_recv()
        other = part(esib)
        fbs[first:last] = (away + term(*other, 1, 0)).reshape(last - first, ROWS, quarter)
        fb_copy(first, last).start()
        out[first * ROWS : last * ROWS] = term(*mine, 0, 1) + term(*other, 1, 1)

    def turn(j):
        clear()

        @pl.when(j >= slots)
        def _():
            pl.semaphore_wait(s_free, 1)

        steps(j, 0, nkc + 1)
        scatter(j)
        loop(0, nkc, lambda k: f_copy(j, k).wait_send())

        @pl.when(j + slots < ng)
        def _():
            pl.semaphore_signal(x_free, inc=1, device_id=(far, col), device_id_type=MESH)
            pl.semaphore_signal(s_free, inc=1, device_id=(sib, col), device_id_type=MESH)

        @pl.when((j >= 1) & (j + slots - 1 < ng))
        def _():
            pl.semaphore_wait(x_free, 1)

            def again(k):
                x_copy(j - 1, k).wait_send()
                x_copy(j + slots - 1, k).start()

            loop(0, nkc, again)

        @pl.when((j >= 3) & (j - 2 < npeer))
        def _():
            relay(j - 2)

        @pl.when(j >= 1)
        def _():
            gather(j - 1)

    last = ng - 1
    if last:
        loop(0, last, turn)
    loop(max(1, last - 2), npeer, relay)

    for copy in c_copies(0):
        copy.wait_recv()
    loop(1, npeer, lambda p: r_copy(p).wait_recv())
    for copy in local:
        copy.wait()
    block = ct.shape[1]

    def c_load(i, slot):
        return pltpu.make_async_copy(cbuf.at[pl.ds(i * block, block)], ct.at[slot], ct_sem.at[slot])

    c_load(0, 0).start()

    @functools.partial(loop, 0, cols // block)
    def _(i):
        slot = lax.rem(i, 2)

        @pl.when(i + 1 < cols // block)
        def _():
            c_load(i + 1, 1 - slot).start()

        c_load(i, slot).wait()
        here = pl.ds(pl.multiple_of(i * block * cr, block * cr), block * cr)
        for q in range(2):
            for h in range(2):
                high, low = halves(ct[slot, :, q, h].reshape(block * cr, quarter))
                chi[q, here, h * quarter : (h + 1) * quarter] = high
                clo[q, here, h * quarter : (h + 1) * quarter] = low

    batches = []
    if last > 1:
        bias(0, last - 1)
        batches.append((0, last - 1))
    clear()
    if last >= slots:
        pl.semaphore_wait(s_free, 1)
    middle = (nkc + 1) // 2
    steps(last, 0, middle)
    if last:
        gather(last - 1)
        bias(last - 1, last)
        batches.append((last - 1, last))
    steps(last, middle, nkc + 1)
    scatter(last)
    gather(last)
    bias(last, ng)
    batches.append((last, ng))
    for first, end in batches:
        fb_copy(first, end).wait_recv()
        out[first * ROWS : end * ROWS] += fbl[first:end].reshape((end - first) * ROWS, quarter)

    loop(0, nkc, lambda k: f_copy(last, k).wait_send())
    for j in range(max(0, ng - slots), ng):
        loop(0, nkc, functools.partial(lambda j, k: x_copy(j, k).wait_send(), j))
    loop(0, nkc, lambda k: n_copy(k).wait_send())
    for copy in to_sib:
        copy.wait_send()

    def sent(p):
        for copy in c_copies(p):
            copy.wait_send()

    loop(0, npeer, sent)
    loop(1, npeer, lambda p: r_copy(p).wait_send())

    def e_sent(j):
        loop(1, cols, lambda t: e_copy(j, t).wait_send())
        es_copy(j).wait_send()

    loop(0, ng, e_sent)
    for first, end in batches:
        fb_copy(first, end).wait_send()


def per_device(green_vectors, amplitudes, cholesky):
    rows, cols = lax.axis_size("row"), lax.axis_size("col")
    held, pairs = green_vectors.shape
    depth = amplitudes.shape[0]
    cr, quarter = cholesky.shape[0], cholesky.shape[1] // rows
    if rows != 4 or cols % 2 or rows * held % (cols * ROWS):
        raise ValueError("unexpected mesh")
    wpo = rows * held // cols
    opr, ng = held // wpo, wpo // ROWS
    chunk = min(CHUNK, pairs)
    nkc, nk = pairs // chunk, 2
    slots = min(SLOTS, ng)
    n = 2 * opr * ROWS
    block = max(1, 16 // cr)
    dma = pltpu.SemaphoreType.DMA
    vmem = pltpu.VMEM
    scratch = [
        vmem((nkc, depth, chunk), BF16),
        vmem((nkc, depth, chunk), BF16),
        vmem((2, cols * cr, 2 * quarter), BF16),
        vmem((2, cols * cr, 2 * quarter), BF16),
        vmem((slots, opr, ROWS, pairs), F32),
        vmem((slots, opr, ROWS, pairs), F32),
        vmem((2, depth, TILE), F32),
        vmem((2, 2, opr, ng, ROWS, TILE), F32),
        vmem((2, block, 2, 2, cr, quarter), F32),
        vmem((2 * held, depth), F32),
        vmem((2 * n, depth), F32),
        vmem((n, depth), F32),
        vmem((ng, cols, ROWS, depth), F32),
        vmem((ng, cols, ROWS, depth), F32),
        vmem((ng, ROWS, depth), F32),
        vmem((ng, ROWS, depth), F32),
        vmem((ng, ROWS, quarter), F32),
        vmem((ng, ROWS, quarter), F32),
        dma((slots, nkc)),
        dma((slots, nkc)),
        dma((slots, nkc)),
        dma((slots, nkc)),
        pltpu.SemaphoreType.REGULAR,
        pltpu.SemaphoreType.REGULAR,
        dma((nkc,)),
        dma((nkc,)),
        dma((2, 3)),
        dma((2,)),
        dma((2,)),
        dma((2,)),
        dma((cols // 2, 3)),
        dma((cols // 2, 3)),
        dma((cols // 2,)),
        dma((cols // 2,)),
        dma((2,)),
        dma((ng, cols)),
        dma((ng, cols)),
        dma((ng,)),
        dma((ng,)),
        dma((ng,)),
        dma((ng,)),
    ]
    hbm = pl.BlockSpec(memory_space=pl.ANY)
    return pl.pallas_call(
        functools.partial(kernel, rows, cols),
        out_shape=(
            jax.ShapeDtypeStruct((wpo, quarter), F32),
            jax.ShapeDtypeStruct((opr, ng, ROWS, pairs), F32),
            jax.ShapeDtypeStruct((cols, 2, 2, cr, quarter), F32),
        ),
        in_specs=[hbm] * 3,
        out_specs=(pl.BlockSpec(memory_space=pltpu.VMEM), hbm, hbm),
        scratch_shapes=scratch,
        compiler_params=pltpu.CompilerParams(
            collective_id=0, has_side_effects=True, vmem_limit_bytes=67_043_328
        ),
    )(green_vectors.reshape(opr, ng, ROWS, pairs), amplitudes, cholesky)[0]


def solution(mesh):
    placed = (P("row", "col"), P("row", "col"), P(("row", "col"), None))
    return jax.shard_map(
        per_device, mesh=mesh, in_specs=placed, out_specs=P("col", "row"), check_vma=False
    )
```

time: 255 us -> 239 us (0.937)
  Pallas kernels: 41.3 us -> 235 us
  waiting for transfers between devices: 129 us -> 0 us
  matrix products: 49.7 us -> 0 us
  between operations: 13.5 us -> 0.01 us
  starting transfers between devices: 10.4 us -> 0 us
  local copies, waits for them, and re-layouts: 10.6 us -> 1.67 us
    pallas_call x1, Pallas kernels: 41.3 us -> 235 us  [per_device(): pl.pallas_call(functools.partial(kernel, rows, cols), out_shape=(jax.Shap...]
    ppermute x9 -> x0, waiting for transfers between devices: 129 us -> none  [the longest x4 127 us: far(): lax.ppermute(piece, 'row', [(i, (i + hop) % rows) for i in range(rows)])]
    dot_general x5 -> x0, matrix products: 49.7 us -> none  [three_pass(): lax.dot_general(left, right, (dims, ((), ())), precision=lax.Precision.HI...]
    ppermute x9 -> x0, starting transfers between devices: 10.4 us -> none  [the longest x4 5.81 us: cross(): return [lax.ppermute(piece, 'row', sibling) for piece in pieces]]
    slice x4 -> x0, local copies, waits for them, and re-layouts: 9.67 us -> none  [part(): return lax.slice_in_dim(array, cuts[c], cuts[c + 1], axis=1)]
  transfers between devices with their start and end apart: 10 -> 0, of which waited for: 5 -> 0; matrix products, arithmetic and copies ran while one was open for 22% -> 0% of each run, Pallas kernels for 0% -> 0%
where the time goes in v1:
time: 239 us; the launch traced here: 237 us
  Pallas kernels  235 us (98%)
    pallas_call x1, Pallas kernels, per_device(): pl.pallas_call(functools.partial(kernel, rows, cols), out_shape=(jax.Shap...  235 us

profile of v1, /device:TPU:13, one launch (start us, length us, event | category | flops | bytes accessed | tf_op | source)
XLA Modules:
  0.0 237.0 jit_solution(14983397908592400955)
XLA Ops:
  0.0 235.3 %shard_map.37 = (f32[64,1024]{1,0:T(8,128)}, f32[2,8,8,16384]{3,2,1,0:T(8,128)}, f32[8,2,2,64,1024]{4,3,2,1,0:T(8,128)}) custom-call(f32[2,8,8,16384]{3,2,1,0:T(8,128)} %bitcast.1, f32[512,16384]{1,0:T(8,128)} %a.1, f32[64,4096]{1,0:T(8,128)} %c.1), custom_call_target="tpu_custom_call" | custom-call | tf_op jit(solution)/shard_map/pallas_call | solution.py:445
  235.3 1.7 copy.5

commit v2 on v1

--- a/solution.py
+++ b/solution.py
@@ -13,6 +13,7 @@
 SLOTS = 4
 CHUNK = 2048
 TILE = 512
+RELAYS = (1, 3)
 
 
 def halves(x):
@@ -134,8 +135,9 @@
             remote(cbuf.at[col, 1], cbuf.at[col, 1], c_send.at[p, 2], c_recv.at[p, 2], target),
         ]
 
-    def r_copy(p):
-        return remote(cbuf.at[c_source(p)], cbuf.at[c_source(p)], r_send.at[p], r_recv.at[p], (row, pal))
+    def r_copy(p, q):
+        piece = cbuf.at[c_source(p), q]
+        return remote(piece, piece, r_send.at[p, q], r_recv.at[p, q], (row, pal))
 
     for copy in to_sib:
         copy.start()
@@ -154,10 +156,14 @@
         copy.wait_recv()
     loop(0, npeer, lambda p: c_copies(p)[2].start())
 
-    def relay(p):
-        for copy in c_copies(p):
-            copy.wait_recv()
-        r_copy(p).start()
+    def relay(q):
+        def one(p):
+            copies = c_copies(p)
+            for copy in copies[2:] if q else copies[:2]:
+                copy.wait_recv()
+            r_copy(p, q).start()
+
+        loop(1, npeer, one)
 
     eown[...] = jnp.zeros_like(eown)
     n_copy(0).wait_recv()
@@ -262,13 +268,13 @@
             return pair[:m] + (pair[m:] + dot_nn(high, clo[q, :, here]))
 
         mine = part(esend)
-        away = term(*mine, 0, 0)
+        away, kept = term(*mine, 0, 0), term(*mine, 0, 1)
         for j in range(first, last):
             es_copy(j).wait_recv()
         other = part(esib)
         fbs[first:last] = (away + term(*other, 1, 0)).reshape(last - first, ROWS, quarter)
         fb_copy(first, last).start()
-        out[first * ROWS : last * ROWS] = term(*mine, 0, 1) + term(*other, 1, 1)
+        out[first * ROWS : last * ROWS] = kept + term(*other, 1, 1)
 
     def turn(j):
         clear()
@@ -296,22 +302,23 @@
 
             loop(0, nkc, again)
 
-        @pl.when((j >= 3) & (j - 2 < npeer))
-        def _():
-            relay(j - 2)
-
-        @pl.when(j >= 1)
-        def _():
-            gather(j - 1)
+        for q in range(2):
+
+            @pl.when(j == RELAYS[q])
+            def _():
+                relay(q)
 
     last = ng - 1
     if last:
         loop(0, last, turn)
-    loop(max(1, last - 2), npeer, relay)
+    for q in range(2):
+        if RELAYS[q] >= last:
+            relay(q)
 
     for copy in c_copies(0):
         copy.wait_recv()
-    loop(1, npeer, lambda p: r_copy(p).wait_recv())
+    for q in range(2):
+        loop(1, npeer, lambda p: r_copy(p, q).wait_recv())
     for copy in local:
         copy.wait()
     block = ct.shape[1]
@@ -339,6 +346,7 @@
 
     batches = []
     if last > 1:
+        loop(0, last - 1, gather)
         bias(0, last - 1)
         batches.append((0, last - 1))
     clear()
@@ -371,7 +379,8 @@
             copy.wait_send()
 
     loop(0, npeer, sent)
-    loop(1, npeer, lambda p: r_copy(p).wait_send())
+    for q in range(2):
+        loop(1, npeer, lambda p: r_copy(p, q).wait_send())
 
     def e_sent(j):
         loop(1, cols, lambda t: e_copy(j, t).wait_send())
@@ -431,8 +440,8 @@
         dma((2,)),
         dma((cols // 2, 3)),
         dma((cols // 2, 3)),
-        dma((cols // 2,)),
-        dma((cols // 2,)),
+        dma((cols // 2, 2)),
+        dma((cols // 2, 2)),
         dma((2,)),
         dma((ng, cols)),
         dma((ng, cols)),

time: 239 us -> 206 us (0.86)
  Pallas kernels: 235 us -> 202 us
    pallas_call x1, Pallas kernels: 235 us -> 202 us  [per_device(): pl.pallas_call(functools.partial(kernel, rows, cols), out_shape=(jax.Shap...]
where the time goes in v2:
time: 206 us; the launch traced here: 204 us
  Pallas kernels  202 us (98%)
    pallas_call x1, Pallas kernels, per_device(): pl.pallas_call(functools.partial(kernel, rows, cols), out_shape=(jax.Shap...  202 us

profile of v2, /device:TPU:13, one launch (start us, length us, event | category | flops | bytes accessed | tf_op | source)
XLA Modules:
  0.0 203.8 jit_solution(5430104388424743016)
XLA Ops:
  0.0 202.1 %shard_map.37 = (f32[64,1024]{1,0:T(8,128)}, f32[2,8,8,16384]{3,2,1,0:T(8,128)}, f32[8,2,2,64,1024]{4,3,2,1,0:T(8,128)}) custom-call(f32[2,8,8,16384]{3,2,1,0:T(8,128)} %bitcast.1, f32[512,16384]{1,0:T(8,128)} %a.1, f32[64,4096]{1,0:T(8,128)} %c.1), custom_call_target="tpu_custom_call" | custom-call | tf_op jit(solution)/shard_map/pallas_call | solution.py:454
  202.1 1.7 copy.5

commit v3 on v2

--- a/solution.py
+++ b/solution.py
@@ -10,8 +10,10 @@
 MESH = pl.DeviceIdType.MESH
 F32, BF16 = jnp.float32, jnp.bfloat16
 ROWS = 8
+LATE = 2
 SLOTS = 4
 CHUNK = 2048
+WIDE = 4
 TILE = 512
 RELAYS = (1, 3)
 
@@ -32,7 +34,7 @@
 def kernel(
     rows, cols, g, a, c, out, near, cbuf,
     ahi, alo, chi, clo, xs, ss, at, gt, ct, eown, acc, acc2, stage, eland, esend, esib, fbs, fbl,
-    x_send, x_recv, f_send, f_recv, x_free, s_free, n_send, n_recv, ld,
+    x_send, x_recv, f_send, f_recv, x_free, s_free, up, down, across, n_send, n_recv, ld,
     cl_sem, cs_send, cs_recv, c_send, c_recv, r_send, r_recv, ct_sem,
     e_send, e_recv, es_send, es_recv, fb_send, fb_recv,
 ):
@@ -65,12 +67,17 @@
         lax.fori_loop(lo, hi, step, 0)
 
     barrier = pltpu.get_barrier_semaphore()
-    pl.semaphore_signal(barrier, inc=1, device_id=(far, col), device_id_type=MESH)
-    pl.semaphore_signal(barrier, inc=1, device_id=(sib, col), device_id_type=MESH)
-
-    @functools.partial(loop, 1, cols)
-    def _(t):
-        pl.semaphore_signal(barrier, inc=1, device_id=(row, lax.rem(col + t, cols)), device_id_type=MESH)
+    place, places = col // 2, cols // 2
+    below, above = place > 0, place < places - 1
+
+    def signal(semaphore, to_row, to_col):
+        pl.semaphore_signal(semaphore, inc=1, device_id=(to_row, to_col), device_id_type=MESH)
+
+    signal(barrier, far, col)
+    signal(barrier, sib, col)
+    signal(barrier, row, pal)
+    pl.when(below)(lambda: signal(barrier, row, col - 2))
+    pl.when(above)(lambda: signal(barrier, row, col + 2))
 
     def load(i, slot):
         at_pairs = pl.ds(pl.multiple_of(i * tile, tile), tile)
@@ -88,29 +95,52 @@
         )
         for h, quarter_of in enumerate((far, row))
     ]
-    pl.semaphore_wait(barrier, cols + 1)
+    pl.semaphore_wait(barrier, 3 + jnp.where(below, 1, 0) + jnp.where(above, 1, 0))
 
     def pairs_of(k):
         return pl.ds(pl.multiple_of(k * chunk, chunk), chunk)
 
-    def x_copy(j, k):
-        slot = lax.rem(j, slots)
+    last = ng - 1
+    early = max(0, ng - LATE)
+    wide = min(WIDE, nkc)
+    half = chunk // 2
+
+    def cut(kind, k):
+        if kind == "wide":
+            return pl.ds(pl.multiple_of(k * wide * chunk, wide * chunk), wide * chunk)
+        if kind == "half":
+            return pl.ds(pl.multiple_of((nkc - 1) * chunk + (k - nkc + 1) * half, half), half)
+        return pairs_of(k)
+
+    def x_copy(j, k, kind="chunk"):
+        slot, here = lax.rem(j, slots), cut(kind, k)
         return remote(
-            g.at[:, j, :, pairs_of(k)], xs.at[slot, :, :, pairs_of(k)],
-            x_send.at[slot, k], x_recv.at[slot, k], (far, col),
+            g.at[:, j, :, here], xs.at[slot, :, :, here], x_send.at[slot, k], x_recv.at[slot, k], (far, col)
         )
 
-    def f_copy(j, k):
-        slot = lax.rem(j, slots)
+    def f_copy(j, k, kind="chunk"):
+        slot, here = lax.rem(j, slots), cut(kind, k)
         return remote(
-            xs.at[slot, :, :, pairs_of(k)], ss.at[slot, :, :, pairs_of(k)],
-            f_send.at[slot, k], f_recv.at[slot, k], (sib, col),
+            xs.at[slot, :, :, here], ss.at[slot, :, :, here], f_send.at[slot, k], f_recv.at[slot, k], (sib, col)
         )
+
+    def each(j, body):
+        if isinstance(j, int) and j == last:
+            loop(0, nkc - 1, lambda k: body(k, "chunk"))
+            body(nkc - 1, "half")
+            body(nkc, "half")
+        elif isinstance(j, int) and j >= early:
+            loop(0, nkc, lambda k: body(k, "chunk"))
+        else:
+            loop(0, nkc // wide, lambda k: body(k, "wide"))
+
+    def start_far(j):
+        each(j, lambda k, kind: x_copy(j, k, kind).start())
 
     def n_copy(k):
         return remote(g.at[:, :, :, pairs_of(k)], near.at[:, :, :, pairs_of(k)], n_send.at[k], n_recv.at[k], (sib, col))
 
-    loop(0, nkc, lambda k: x_copy(0, k).start())
+    start_far(0)
     n_copy(0).start()
 
     def c_quarter(m):
@@ -147,11 +177,25 @@
         for copy in c_copies(p)[:2]:
             copy.start()
 
-    loop(0, npeer, send_own)
+    for j in range(1, min(slots, ng)):
+        start_far(j)
     for copy in local:
         copy.start()
-    for j in range(1, min(slots, ng)):
-        loop(0, nkc, functools.partial(lambda j, k: x_copy(j, k).start(), j))
+
+    @pl.when(below)
+    def _():
+        pl.semaphore_wait(up, 1)
+
+    pl.when(above)(lambda: signal(up, row, col + 2))
+
+    @pl.when(above)
+    def _():
+        pl.semaphore_wait(down, 1)
+
+    pl.when(below)(lambda: signal(down, row, col - 2))
+    signal(across, row, pal)
+    pl.semaphore_wait(across, 1)
+    loop(0, npeer, send_own)
     for copy in to_sib:
         copy.wait_recv()
     loop(0, npeer, lambda p: c_copies(p)[2].start())
@@ -194,30 +238,37 @@
             pair = dot_nt(jnp.concatenate([g_high, g_low], axis=0), high)
             eown[...] += pair[: 2 * held] + (pair[2 * held :] + dot_nt(g_high, low))
 
+    def arrive(j, k, kind):
+        x_copy(j, k, kind).wait_recv()
+        f_copy(j, k, kind).start()
+
+    def multiply(j, here, left, low_left):
+        slot, size = lax.rem(j, slots), left.shape[1]
+        block = jnp.concatenate(
+            [xs[slot, :, :, here].reshape(n // 2, size), ss[slot, :, :, here].reshape(n // 2, size)], axis=0
+        )
+        high, low = halves(block)
+        acc[...] += dot_nt(jnp.concatenate([high, low], axis=0), left)
+        acc2[...] += dot_nt(high, low_left)
+
+    def consume(j, k, kind):
+        f_copy(j, k, kind).wait_recv()
+        if kind == "wide":
+            loop(k * wide, (k + 1) * wide, lambda b: multiply(j, pairs_of(b), ahi[b], alo[b]))
+        elif kind == "half":
+            here = slice((k - nkc + 1) * half, (k - nkc + 2) * half)
+            multiply(j, cut(kind, k), ahi[nkc - 1, :, here], alo[nkc - 1, :, here])
+        else:
+            multiply(j, pairs_of(k), ahi[k], alo[k])
+
     def steps(j, lo, hi):
-        slot = lax.rem(j, slots)
-
         @functools.partial(loop, lo, hi)
         def _(k):
-            @pl.when(k < nkc)
-            def _():
-                x_copy(j, k).wait_recv()
-                f_copy(j, k).start()
+            arrive(j, k, "chunk")
 
             @pl.when(k > 0)
             def _():
-                f_copy(j, k - 1).wait_recv()
-                here = pairs_of(k - 1)
-                block = jnp.concatenate(
-                    [
-                        xs[slot, :, :, here].reshape(n // 2, chunk),
-                        ss[slot, :, :, here].reshape(n // 2, chunk),
-                    ],
-                    axis=0,
-                )
-                high, low = halves(block)
-                acc[...] += dot_nt(jnp.concatenate([high, low], axis=0), ahi[k - 1])
-                acc2[...] += dot_nt(high, alo[k - 1])
+                consume(j, k - 1, "chunk")
 
     def clear():
         acc[...] = jnp.zeros_like(acc)
@@ -276,6 +327,13 @@
         fb_copy(first, last).start()
         out[first * ROWS : last * ROWS] = kept + term(*other, 1, 1)
 
+    def pass_on(j):
+        for q in range(2):
+
+            @pl.when(j == RELAYS[q])
+            def _():
+                relay(q)
+
     def turn(j):
         clear()
 
@@ -283,36 +341,34 @@
         def _():
             pl.semaphore_wait(s_free, 1)
 
-        steps(j, 0, nkc + 1)
+        def one(k):
+            arrive(j, k, "wide")
+            consume(j, k, "wide")
+
+        loop(0, nkc // wide, one)
         scatter(j)
-        loop(0, nkc, lambda k: f_copy(j, k).wait_send())
+        each(j, lambda k, kind: f_copy(j, k, kind).wait_send())
 
         @pl.when(j + slots < ng)
         def _():
-            pl.semaphore_signal(x_free, inc=1, device_id=(far, col), device_id_type=MESH)
-            pl.semaphore_signal(s_free, inc=1, device_id=(sib, col), device_id_type=MESH)
-
-        @pl.when((j >= 1) & (j + slots - 1 < ng))
+            signal(x_free, far, col)
+            signal(s_free, sib, col)
+
+        later = j + slots - 1
+
+        @pl.when((j >= 1) & (later < ng))
         def _():
             pl.semaphore_wait(x_free, 1)
-
-            def again(k):
-                x_copy(j - 1, k).wait_send()
-                x_copy(j + slots - 1, k).start()
-
-            loop(0, nkc, again)
-
-        for q in range(2):
-
-            @pl.when(j == RELAYS[q])
-            def _():
-                relay(q)
-
-    last = ng - 1
-    if last:
-        loop(0, last, turn)
+            each(j, lambda k, kind: x_copy(j - 1, k, kind).wait_send())
+            pl.when(later < early)(lambda: start_far(later))
+            for m in range(max(slots, early), ng):
+                pl.when(later == m)(functools.partial(start_far, m))
+
+        pass_on(j)
+
+    loop(0, early, turn)
     for q in range(2):
-        if RELAYS[q] >= last:
+        if RELAYS[q] >= early:
             relay(q)
 
     for copy in c_copies(0):
@@ -345,31 +401,44 @@
                 clo[q, here, h * quarter : (h + 1) * quarter] = low
 
     batches = []
-    if last > 1:
-        loop(0, last - 1, gather)
-        bias(0, last - 1)
-        batches.append((0, last - 1))
-    clear()
-    if last >= slots:
-        pl.semaphore_wait(s_free, 1)
-    middle = (nkc + 1) // 2
-    steps(last, 0, middle)
-    if last:
-        gather(last - 1)
-        bias(last - 1, last)
-        batches.append((last - 1, last))
-    steps(last, middle, nkc + 1)
-    scatter(last)
-    gather(last)
-    bias(last, ng)
-    batches.append((last, ng))
+
+    def finish(end):
+        first = batches[-1][1] if batches else 0
+        if first < end:
+            loop(first, end, gather)
+            bias(first, end)
+            batches.append((first, end))
+
+    finish(early - 1)
+    for j in range(early, ng):
+        clear()
+        if j >= slots:
+            pl.semaphore_wait(s_free, 1)
+        if j < last:
+            steps(j, 0, nkc)
+            consume(j, nkc - 1, "chunk")
+        else:
+            middle = (nkc - 1) // 2
+            steps(j, 0, middle)
+            finish(last)
+            steps(j, middle, nkc - 1)
+            arrive(j, nkc - 1, "half")
+            if nkc > 1:
+                consume(j, nkc - 2, "chunk")
+            arrive(j, nkc, "half")
+            consume(j, nkc - 1, "half")
+            consume(j, nkc, "half")
+        scatter(j)
+        if j < last:
+            each(j, functools.partial(lambda j, k, kind: f_copy(j, k, kind).wait_send(), j))
+    finish(ng)
     for first, end in batches:
         fb_copy(first, end).wait_recv()
         out[first * ROWS : end * ROWS] += fbl[first:end].reshape((end - first) * ROWS, quarter)
 
-    loop(0, nkc, lambda k: f_copy(last, k).wait_send())
+    each(last, lambda k, kind: f_copy(last, k, kind).wait_send())
     for j in range(max(0, ng - slots), ng):
-        loop(0, nkc, functools.partial(lambda j, k: x_copy(j, k).wait_send(), j))
+        each(j, functools.partial(lambda j, k, kind: x_copy(j, k, kind).wait_send(), j))
     loop(0, nkc, lambda k: n_copy(k).wait_send())
     for copy in to_sib:
         copy.wait_send()
@@ -426,12 +495,11 @@
         vmem((ng, ROWS, depth), F32),
         vmem((ng, ROWS, quarter), F32),
         vmem((ng, ROWS, quarter), F32),
-        dma((slots, nkc)),
-        dma((slots, nkc)),
-        dma((slots, nkc)),
-        dma((slots, nkc)),
-        pltpu.SemaphoreType.REGULAR,
-        pltpu.SemaphoreType.REGULAR,
+        dma((slots, nkc + 1)),
+        dma((slots, nkc + 1)),
+        dma((slots, nkc + 1)),
+        dma((slots, nkc + 1)),
+        *[pltpu.SemaphoreType.REGULAR] * 5,
         dma((nkc,)),
         dma((nkc,)),
         dma((2, 3)),

time: 206 us -> 205 us (level)
  no operation moved by 1% of the time
where the time goes in v3:
time: 205 us; the launch traced here: 202 us
  Pallas kernels  200 us (98%)
    pallas_call x1, Pallas kernels, per_device(): pl.pallas_call(functools.partial(kernel, rows, cols), out_shape=(jax.Shap...  200 us

profile of v3, /device:TPU:13, one launch (start us, length us, event | category | flops | bytes accessed | tf_op | source)
XLA Modules:
  0.0 202.1 jit_solution(732717274476475777)
XLA Ops:
  0.0 200.4 %shard_map.37 = (f32[64,1024]{1,0:T(8,128)}, f32[2,8,8,16384]{3,2,1,0:T(8,128)}, f32[8,2,2,64,1024]{4,3,2,1,0:T(8,128)}) custom-call(f32[2,8,8,16384]{3,2,1,0:T(8,128)} %bitcast.1, f32[512,16384]{1,0:T(8,128)} %a.1, f32[64,4096]{1,0:T(8,128)} %c.1), custom_call_target="tpu_custom_call" | custom-call | tf_op jit(solution)/shard_map/pallas_call | solution.py:522
  200.4 1.7 copy.5

commit v4 on v3

--- a/solution.py
+++ b/solution.py
@@ -13,7 +13,7 @@
 LATE = 2
 SLOTS = 4
 CHUNK = 2048
-WIDE = 4
+WIDE = 2
 TILE = 512
 RELAYS = (1, 3)
 
@@ -281,16 +281,27 @@
     def es_copy(j):
         return remote(esend.at[j], esib.at[j], es_send.at[j], es_recv.at[j], (sib, col))
 
-    def scatter(j):
+    def send(j, here):
+        def one(t):
+            owner = lax.rem(col + t, cols) // opr
+            pl.when((owner // 2 == row // 2) == here)(lambda: e_copy(j, t).start())
+
+        loop(1, cols, one)
+
+    def scatter_own(j):
         for i in range(opr):
             mine = pl.multiple_of(i * wpo + j * ROWS, ROWS)
             stage[j, row * opr + i] = eown[pl.ds(mine, ROWS)]
             stage[j, sib * opr + i] = eown[pl.ds(held + mine, ROWS)]
+        send(j, True)
+
+    def scatter_far(j):
+        for i in range(opr):
             at_far, at_sib = slice(i * ROWS, (i + 1) * ROWS), slice((opr + i) * ROWS, (opr + i + 1) * ROWS)
             for owner, here in ((far, at_far), (far_sib, at_sib)):
                 below = slice(n + here.start, n + here.stop)
                 stage[j, owner * opr + i] = acc[here] + (acc[below] + acc2[here])
-        loop(1, cols, lambda t: e_copy(j, t).start())
+        send(j, False)
 
     def gather(j):
         def add(t, total):
@@ -324,7 +335,8 @@
             es_copy(j).wait_recv()
         other = part(esib)
         fbs[first:last] = (away + term(*other, 1, 0)).reshape(last - first, ROWS, quarter)
-        fb_copy(first, last).start()
+        if last == ng:
+            fb_copy(first, last).start()
         out[first * ROWS : last * ROWS] = kept + term(*other, 1, 1)
 
     def pass_on(j):
@@ -342,11 +354,17 @@
             pl.semaphore_wait(s_free, 1)
 
         def one(k):
-            arrive(j, k, "wide")
-            consume(j, k, "wide")
-
-        loop(0, nkc // wide, one)
-        scatter(j)
+            @pl.when(k < nkc // wide)
+            def _():
+                arrive(j, k, "wide")
+
+            @pl.when(k > 0)
+            def _():
+                consume(j, k - 1, "wide")
+
+        loop(0, nkc // wide + 1, one)
+        scatter_own(j)
+        scatter_far(j)
         each(j, lambda k, kind: f_copy(j, k, kind).wait_send())
 
         @pl.when(j + slots < ng)
@@ -421,14 +439,19 @@
             middle = (nkc - 1) // 2
             steps(j, 0, middle)
             finish(last)
+            scatter_own(j)
             steps(j, middle, nkc - 1)
             arrive(j, nkc - 1, "half")
             if nkc > 1:
                 consume(j, nkc - 2, "chunk")
             arrive(j, nkc, "half")
+            for pair in batches:
+                fb_copy(*pair).start()
             consume(j, nkc - 1, "half")
             consume(j, nkc, "half")
-        scatter(j)
+        if j < last:
+            scatter_own(j)
+        scatter_far(j)
         if j < last:
             each(j, functools.partial(lambda j, k, kind: f_copy(j, k, kind).wait_send(), j))
     finish(ng)

time: 205 us -> 205 us (level)
  no operation moved by 1% of the time
where the time goes in v4:
time: 205 us; the launch traced here: 202 us
  Pallas kernels  200 us (98%)
    pallas_call x1, Pallas kernels, per_device(): pl.pallas_call(functools.partial(kernel, rows, cols), out_shape=(jax.Shap...  200 us

profile of v4, /device:TPU:13, one launch (start us, length us, event | category | flops | bytes accessed | tf_op | source)
XLA Modules:
  0.0 202.0 jit_solution(2521998738008083443)
XLA Ops:
  0.0 200.3 %shard_map.37 = (f32[64,1024]{1,0:T(8,128)}, f32[2,8,8,16384]{3,2,1,0:T(8,128)}, f32[8,2,2,64,1024]{4,3,2,1,0:T(8,128)}) custom-call(f32[2,8,8,16384]{3,2,1,0:T(8,128)} %bitcast.1, f32[512,16384]{1,0:T(8,128)} %a.1, f32[64,4096]{1,0:T(8,128)} %c.1), custom_call_target="tpu_custom_call" | custom-call | tf_op jit(solution)/shard_map/pallas_call | solution.py:545
  200.3 1.7 copy.5
